TPU v7x, 128 devices: a whole 4x4x4 slice. The times are simulated.
128 devices in a mesh: region: 8 (over y, core), local: 16 (over z, x).
Axes of the slice: x: 4, y: 4, z: 4, core: 2. Of those that a mesh axis runs over, the one named last changes fastest.
Arguments:
- block_flags: int32 [32, 768], P(None, ('region', 'local')), may hold values 0 or 1
- trace: bfloat16 [32, 98304], P(None, ('region', 'local')), may hold values from 0.099609375 to 1
- w_region: bfloat16 [8, 12288, 12288], P('region', None, 'local'), may hold values from -0.0546875 to 0.0546875
- lr_weight: bfloat16 [8, 16, 8, 8, 128, 128], P('region', 'local'), may hold values from -0.1875 to 0.1875
- lr_source: int32 [8, 16, 8, 8], P('region', 'local'), may hold values from 0 to 5
- lr_target: int32 [8, 16, 8, 8], P('region', 'local'), may hold values from 0 to 95
- lr_count: int32 [8, 16, 8], P('region', 'local'), may hold values from 0 to 8, as said below
- g_decay: float32 [98304], P(('region', 'local')), may hold values from 0.5 to 0.97
- v_decay: float32 [98304], P(('region', 'local')), may hold values from 0.4 to 0.95
- g_start: float32 [98304], P(('region', 'local')), may hold values from -6 to 6
- v_start: float32 [98304], P(('region', 'local')), may hold values from -6 to 6
Outputs:
- membrane: float32 [32, 98304], P(None, ('region', 'local'))
- g_final: float32 [98304], P(('region', 'local'))
Inputs may be any that keep to these rules, and one draw needn't show every extreme that they name: lr_count is 0 for a region's own devices, exactly 8 from every device to the next region (d = (r + 1) % 8), and 1 to 8 otherwise.
All inputs are finite; a program needn't handle non-finite values. No bound on the sum of `block_flags` on one device may be relied on, other than what follows from the above.
Results may differ from a plain program's by a relative error of at most 0.0003.
Values may be sent and summed in bfloat16 or wider, within the bound.
A program may use at most 128 MiB of HBM per device.

v0:
```python
import jax
import jax.numpy as jnp
from jax import lax
from jax.sharding import PartitionSpec as P


def local(
    block_flags,
    trace,
    w_region,
    lr_weight,
    lr_source,
    lr_target,
    lr_count,
    g_decay,
    v_decay,
    g_start,
    v_start,
):
    steps = trace.shape[0]
    own_blocks = block_flags.shape[1]
    width = trace.shape[1] // own_blocks
    drive = (
        trace.reshape(steps, own_blocks, width) * block_flags[:, :, None].astype(jnp.bfloat16)
    ).reshape(steps, own_blocks * width)
    weights = w_region[0]
    rows = weights
    inner = jnp.dot(
        lax.all_gather(drive, "local", axis=1, tiled=True), rows, preferred_element_type=jnp.float32
    )
    counts = lr_count[0, 0]
    targets = lr_target[0, 0]
    sources = lr_source[0, 0]
    tiles = lr_weight[0, 0]
    regions = targets.shape[0]
    slots = targets.shape[1]
    blocks = drive.reshape(steps, own_blocks, width)
    chosen = jnp.take(blocks, sources, axis=1)
    partial_value = jnp.einsum("sdci,dcio->dcso", chosen, tiles, preferred_element_type=jnp.float32)
    live = (jnp.arange(slots, dtype=jnp.int32)[None, :] < counts[:, None]).astype(jnp.float32)
    partial_value = partial_value * live[:, :, None, None]
    arrived, arrived_ids = (
        lax.all_to_all(partial_value, "region", split_axis=0, concat_axis=0, tiled=True),
        lax.all_to_all(targets, "region", split_axis=0, concat_axis=0, tiled=True),
    )
    flat = arrived.reshape(regions * slots, steps * width)
    id_flat = arrived_ids.reshape(regions * slots)
    rows = jnp.arange(lax.axis_size("local") * own_blocks, dtype=jnp.int32)
    onehot = (id_flat[None, :] == rows[:, None]).astype(jnp.float32)
    outer = lax.psum_scatter(
        jnp.dot(onehot, flat, precision=lax.Precision.HIGHEST, preferred_element_type=jnp.float32),
        "local",
        scatter_dimension=0,
        tiled=True,
    )
    outer = (
        outer.reshape(own_blocks, steps, width)
        .transpose(1, 0, 2)
        .reshape(steps, own_blocks * width)
    )
    current = inner + outer

    def advance(carry, now):
        g_state, v_state = carry
        g_state = g_decay * g_state + (1.0 - g_decay) * now
        v_state = v_decay * v_state + (1.0 - v_decay) * g_state
        return ((g_state, v_state), v_state)

    (g_last, v_last), membrane = lax.scan(advance, (g_start, v_start), current)
    return (membrane, g_last)


def solution(mesh):
    return jax.shard_map(
        local,
        mesh=mesh,
        in_specs=(
            P(None, ("region", "local")),
            P(None, ("region", "local")),
            P("region", None, "local"),
            P("region", "local", None, None, None, None),
            P("region", "local", None, None),
            P("region", "local", None, None),
            P("region", "local", None),
            P(("region", "local")),
            P(("region", "local")),
            P(("region", "local")),
            P(("region", "local")),
        ),
        out_specs=(P(None, ("region", "local")), P(("region", "local"))),
        check_vma=False,
    )
```

profile of v0, /device:TPU:0, one launch (start us, length us, event | category | flops | bytes accessed | tf_op | source)
XLA Modules:
  0.0 195.3 jit_solution(16240093048172563462)
XLA Ops:
  7.2 4.7 %all-to-all-start = ((s32[8,1,8]{2,1,0:T(1,128)}), s32[8,1,8]{2,1,0:T(1,128)S(1)}, u32[]{:S(2)}, u32[]{:S(2)}) async-start(s32[8,1,8]{2,1,0:T(1,128)} %bitcast.50), calls=%async_computation | async-start | bytes 8192 | tf_op jit(solution)/shard_map/all_to_all | solution.py:44
  11.9 0.7 convert_element_type.12
  12.6 0.7 compare_select_fusion
  13.3 0.8 fusion.18
  14.1 0.9 bitcast_multiply_fusion.1
  15.0 0.7 gather_fusion
  15.7 1.7 fusion.4
  17.4 4.8 %all-to-all-start.1 = ((f32[8,8,32,128]{3,2,1,0:T(8,128)}), f32[8,8,32,128]{3,2,1,0:T(8,128)S(1)}, u32[]{:S(2)}, u32[]{:S(2)}) async-start(f32[8,8,32,128]{3,2,1,0:T(8,128)} %fusion.4), calls=%async_computation.1 | async-start | bytes 2097152 | tf_op jit(solution)/shard_map/all_to_all | solution.py:43
  22.7 0.7 reduce.5
  23.5 14.7 %all-to-all-done.1 = f32[8,8,32,128]{3,2,1,0:T(8,128)S(1)} async-done(((f32[8,8,32,128]{3,2,1,0:T(8,128)}), f32[8,8,32,128]{3,2,1,0:T(8,128)S(1)}, u32[]{:S(2)}, u32[]{:S(2)}) %all-to-all-start.1) | async-done | bytes 1048608 | tf_op jit(solution)/shard_map/all_to_all | solution.py:43
  38.1 2.6 %fusion.10 = f32[96,4096]{1,0:T(8,128)} fusion(f32[8,8,32,128]{3,2,1,0:T(8,128)S(1)} %all-to-all-done.1, s32[64]{0:T(128)S(1)} %eq.15), kind=kOutput, calls=%fused_computation.10 | convolution fusion | flops 301996032 | bytes 2621696 | tf_op jit(solution)/shard_map/dot_general | solution.py:51
  42.3 27.9 %all_gather.3 = bf16[32,12288]{1,0:T(8,128)(2,1)S(1)} all-gather(bf16[32,768]{1,0:T(8,128)(2,1)S(1)} %bitcast_multiply_fusion), channel_id=1, replica_groups=mesh['region'=8,'local'=16] {'local'}, dimensions={1}, use_global_device_ids=true | all-gather | bytes 835584 | tf_op jit(solution)/shard_map/all_gather | solution.py:29
  70.2 61.4 %all-reduce.3.cloned.1.call-done = f32[96,4096]{1,0:T(8,128)} async-done(((f32[96,4096]{1,0:T(8,128)}), f32[96,4096]{1,0:T(8,128)}) %all-reduce.3.cloned.1.call-update) | async-done | bytes 1572880
  131.6 1.0 constant_dynamic-slice_fusion
  132.6 9.6 %fusion.7 = f32[32,768]{1,0:T(8,128)S(1)} fusion(bf16[32,12288]{1,0:T(8,128)(2,1)S(1)} %all_gather.3, bf16[1,12288,768]{2,1,0:T(8,128)(2,1)} %param.15, f32[4,8,6,128]{3,2,1,0:T(8,128)S(1)} %bitcast.48), kind=kOutput, calls=%fused_computation.9 | convolution fusion | flops 604004352 | bytes 19857408 | tf_op jit(solution)/shard_map/dot_general | solution.py:28
  142.3 45.5 %while.14 = (s32[]{:T(128)}, f32[768]{0:T(1024)S(1)}, f32[768]{0:T(1024)S(1)}, f32[32,768]{1,0:T(8,128)}, f32[768]{0:T(1024)S(1)}, /*index=5*/f32[32,768]{1,0:T(8,128)S(1)}, f32[768]{0:T(1024)S(1)}, s32[]{:T(128)}, s32[]{:T(128)}) while((s32[]{:T(128)}, f32[768]{0:T(1024)S(1)}, f32[768]{0:T(1024)S(1)}, f32[32,768]{1,0:T(8,128)}, ...), condition=%wide.region_2.3_spmd, body=%wide.region_1.2_spmd.sunk | while | flops 6146 | bytes 40037 | solution.py:69
  142.4 1.4 dynamic_update_slice.5
  143.8 1.4 dynamic_update_slice.5
  145.2 1.4 dynamic_update_slice.5
  146.7 1.4 dynamic_update_slice.5
  148.1 1.4 dynamic_update_slice.5
  149.5 1.4 dynamic_update_slice.5
  150.9 1.4 dynamic_update_slice.5
  152.4 1.4 dynamic_update_slice.5
  153.8 1.4 dynamic_update_slice.5
  155.2 1.4 dynamic_update_slice.5
  156.6 1.4 dynamic_update_slice.5
  158.0 1.4 dynamic_update_slice.5
  159.5 1.4 dynamic_update_slice.5
  160.9 1.4 dynamic_update_slice.5
  162.3 1.4 dynamic_update_slice.5
  163.7 1.4 dynamic_update_slice.5
  165.2 1.4 dynamic_update_slice.5
  166.6 1.4 dynamic_update_slice.5
  168.0 1.4 dynamic_update_slice.5
  169.4 1.4 dynamic_update_slice.5
  170.8 1.4 dynamic_update_slice.5
  172.3 1.4 dynamic_update_slice.5
  173.7 1.4 dynamic_update_slice.5
  175.1 1.4 dynamic_update_slice.5
  176.5 1.4 dynamic_update_slice.5
  178.0 1.4 dynamic_update_slice.5
  179.4 1.4 dynamic_update_slice.5
  180.8 1.4 dynamic_update_slice.5
  182.2 1.4 dynamic_update_slice.5
  183.6 1.4 dynamic_update_slice.5
  185.1 1.4 dynamic_update_slice.5
  186.5 1.4 dynamic_update_slice.5
  (124 shorter events, 3.3 us)
Async XLA Ops:
  7.2 8.5 %copy-start = (bf16[1,1,8,8,128,128]{5,4,3,2,1,0:T(8,128)(2,1)S(1)}, bf16[1,1,8,8,128,128]{5,4,3,2,1,0:T(8,128)(2,1)}, u32[]{:S(2)}) copy-start(bf16[1,1,8,8,128,128]{5,4,3,2,1,0:T(8,128)(2,1)} %param.16) | copy-start | bytes 6291460
  7.2 10.2 %all-to-all-start = ((s32[8,1,8]{2,1,0:T(1,128)}), s32[8,1,8]{2,1,0:T(1,128)S(1)}, u32[]{:S(2)}, u32[]{:S(2)}) async-start(s32[8,1,8]{2,1,0:T(1,128)} %bitcast.50), calls=%async_computation | async-start | bytes 8192 | tf_op jit(solution)/shard_map/all_to_all | solution.py:44
  17.4 20.8 %all-to-all-start.1 = ((f32[8,8,32,128]{3,2,1,0:T(8,128)}), f32[8,8,32,128]{3,2,1,0:T(8,128)S(1)}, u32[]{:S(2)}, u32[]{:S(2)}) async-start(f32[8,8,32,128]{3,2,1,0:T(8,128)} %fusion.4), calls=%async_computation.1 | async-start | bytes 2097152 | tf_op jit(solution)/shard_map/all_to_all | solution.py:43
  22.2 109.5 %all-reduce.3.cloned.1.call-start = ((), (), s32[]{:S(2)}) async-start(), calls=%async_computation.2 | async-start | bytes 3145728
  23.5 17.4 %copy-start.7 = (u32[128]{0:T(128)S(1)}, u32[128]{0:T(128)}, u32[]{:S(2)}) copy-start(u32[128]{0:T(128)} %constant.38) | copy-start | bytes 1540
  23.5 18.8 %copy-start.2 = (bf16[32,768]{1,0:T(8,128)(2,1)S(1)}, bf16[32,768]{1,0:T(8,128)(2,1)}, u32[]{:S(2)}) copy-start(bf16[32,768]{1,0:T(8,128)(2,1)} %param.14) | copy-start | bytes 147460
  132.6 9.7 %copy-start.1 = (f32[768]{0:T(1024)S(1)}, f32[768]{0:T(1024)}, u32[]{:S(2)}) copy-start(f32[768]{0:T(1024)} %param.23) | copy-start | bytes 9220
  132.6 9.7 %copy-start.4 = (f32[768]{0:T(1024)S(1)}, f32[768]{0:T(1024)}, u32[]{:S(2)}) copy-start(f32[768]{0:T(1024)} %param.22) | copy-start | bytes 9220
  132.6 9.7 %copy-start.5 = (f32[768]{0:T(1024)S(1)}, f32[768]{0:T(1024)}, u32[]{:S(2)}) copy-start(f32[768]{0:T(1024)} %param.20) | copy-start | bytes 9220
  132.6 9.7 %copy-start.6 = (f32[768]{0:T(1024)S(1)}, f32[768]{0:T(1024)}, u32[]{:S(2)}) copy-start(f32[768]{0:T(1024)} %param.21) | copy-start | bytes 9220
  187.9 0.6 copy-start.3
Sparse Core Ops, SparseCore 0:
  40.9 90.7 all-reduce.2
where the time goes:
time: 198 us; the launch traced here: 195 us
  waiting for transfers between devices  76.1 us (38%)
  local copies, waits for them, and re-layouts  48.4 us (24%)
  blocking collectives  27.9 us (14%)
  between operations  14.8 us (7%)
  matrix products  13.9 us (7%)
  starting transfers between devices  9.54 us (5%)
  other arithmetic  4.04 us (2%)
    unnamed x2, waiting for transfers between devices  61.4 us
    dynamic_update_slice x32, local copies, waits for them, and re-layouts, local(): (g_last, v_last), membrane = lax.scan(advance, (g_start, v_start), current)  43.8 us
    all_gather x1, blocking collectives, local(): lax.all_gather(drive, 'local', axis=1, tiled=True)  27.9 us
    all_to_all x1, waiting for transfers between devices, local(): lax.all_to_all(partial_value, 'region', split_axis=0, concat_axis=0, tile...  14.7 us
    dot_general x1, matrix products, local(): jnp.dot(lax.all_gather(drive, 'local', axis=1, tiled=True), rows, preferr...  9.64 us
    all_to_all x1, starting transfers between devices, local(): lax.all_to_all(partial_value, 'region', split_axis=0, concat_axis=0, tile...  4.81 us
    all_to_all x1, starting transfers between devices, local(): lax.all_to_all(targets, 'region', split_axis=0, concat_axis=0, tiled=True)  4.7 us
  transfers between devices with their start and end apart: 3, of which 2 were waited for; matrix products, arithmetic and copies ran while one was open for 4% of the time, Pallas kernels for 0%

commit v1 on v0

--- a/solution.py
+++ b/solution.py
@@ -2,6 +2,22 @@
 import jax.numpy as jnp
 from jax import lax
 from jax.sharding import PartitionSpec as P
+
+
+def pairwise_exchange(array, axis, split, join):
+    ways, here = (lax.axis_size(axis), lax.axis_index(axis))
+    width = array.shape[split] // ways
+    shape = list(array.shape)
+    shape[split] = width
+    height = shape[join]
+    shape[join] = height * ways
+    full = jnp.zeros(shape, array.dtype)
+    for mask in range(ways):
+        part = lax.dynamic_slice_in_dim(array, (here ^ mask) * width, width, axis=split)
+        if mask:
+            part = lax.ppermute(part, axis, [(d, d ^ mask) for d in range(ways)])
+        full = lax.dynamic_update_slice_in_dim(full, part, (here ^ mask) * height, axis=join)
+    return full
 
 
 def local(
@@ -41,7 +57,7 @@
     partial_value = partial_value * live[:, :, None, None]
     arrived, arrived_ids = (
         lax.all_to_all(partial_value, "region", split_axis=0, concat_axis=0, tiled=True),
-        lax.all_to_all(targets, "region", split_axis=0, concat_axis=0, tiled=True),
+        pairwise_exchange(targets, "region", 0, 0),
     )
     flat = arrived.reshape(regions * slots, steps * width)
     id_flat = arrived_ids.reshape(regions * slots)

time: 198 us -> 197 us (level)
  starting transfers between devices: 9.54 us -> 14.3 us
  waiting for transfers between devices: 76.1 us -> 71.8 us
    all_to_all x1, waiting for transfers between devices: 14.7 us -> 0.01 us  [local(): lax.all_to_all(partial_value, 'region', split_axis=0, concat_axis=0, tile...]
    ppermute x0 -> x7, starting transfers between devices: none -> 9.75 us  [pairwise_exchange(): part = lax.ppermute(part, axis, [(d, d ^ mask) for d in range(ways)])]
    ppermute x0 -> x7, waiting for transfers between devices: none -> 8.53 us  [pairwise_exchange(): part = lax.ppermute(part, axis, [(d, d ^ mask) for d in range(ways)])]
    all_to_all x1 -> x0, starting transfers between devices: 4.7 us -> none  [local(): lax.all_to_all(targets, 'region', split_axis=0, concat_axis=0, tiled=True)]
  transfers between devices with their start and end apart: 3 -> 9, of which waited for: 2 -> 4; matrix products, arithmetic and copies ran while one was open for 4% -> 1% of each run, Pallas kernels for 0% -> 0%
where the time goes in v1:
time: 197 us; the launch traced here: 194 us
  waiting for transfers between devices  71.8 us (36%)
  local copies, waits for them, and re-layouts  48.1 us (24%)
  blocking collectives  27.4 us (14%)
  between operations  14.8 us (8%)
  starting transfers between devices  14.3 us (7%)
  matrix products  13.9 us (7%)
  other arithmetic  3.53 us (2%)
    unnamed x2, waiting for transfers between devices  63.2 us
    dynamic_update_slice x32, local copies, waits for them, and re-layouts, local(): (g_last, v_last), membrane = lax.scan(advance, (g_start, v_start), current)  43.8 us
    all_gather x1, blocking collectives, local(): lax.all_gather(drive, 'local', axis=1, tiled=True)  27.4 us
    ppermute x7, starting transfers between devices, pairwise_exchange(): part = lax.ppermute(part, axis, [(d, d ^ mask) for d in range(ways)])  9.75 us
    dot_general x1, matrix products, local(): jnp.dot(lax.all_gather(drive, 'local', axis=1, tiled=True), rows, preferr...  9.64 us
    ppermute x7, waiting for transfers between devices, pairwise_exchange(): part = lax.ppermute(part, axis, [(d, d ^ mask) for d in range(ways)])  8.53 us
    all_to_all x1, starting transfers between devices, local(): lax.all_to_all(partial_value, 'region', split_axis=0, concat_axis=0, tile...  4.56 us
  transfers between devices with their start and end apart: 9, of which 4 were waited for; matrix products, arithmetic and copies ran while one was open for 1% of the time, Pallas kernels for 0%

profile of v1, /device:TPU:0, one launch (start us, length us, event | category | flops | bytes accessed | tf_op | source)
XLA Modules:
  0.0 194.5 jit_solution(17237342494453984370)
XLA Ops:
  7.2 0.8 convert_element_type.12
  9.6 0.9 bitcast_multiply_fusion.1
  11.1 1.7 fusion.4
  12.8 4.6 %all-to-all-start = ((f32[8,8,32,128]{3,2,1,0:T(8,128)}), f32[8,8,32,128]{3,2,1,0:T(8,128)S(1)}, u32[]{:S(2)}, u32[]{:S(2)}) async-start(f32[8,8,32,128]{3,2,1,0:T(8,128)} %fusion.4), calls=%async_computation | async-start | bytes 2097152 | tf_op jit(solution)/shard_map/all_to_all | solution.py:59
  18.0 1.7 collective-permute-start.1
  19.7 3.2 %collective-permute-start.3 = (s32[1,8]{1,0:T(1,128)S(1)}, s32[1,8]{1,0:T(1,128)S(1)}, u32[]{:S(2)}, u32[]{:S(2)}) collective-permute-start(s32[1,8]{1,0:T(1,128)S(1)} %get-tuple-element.60), channel_id=1, source_target_pairs={{0,64},{16,80},{32,96},{48,112},{64,0},{80,16},{96,32},{112,48},{1... | collective-permute-start | bytes 104 | tf_op jit(solution)/shard_map/ppermute | solution.py:18
  23.1 3.0 %collective-permute-start.5 = (s32[1,8]{1,0:T(1,128)S(1)}, s32[1,8]{1,0:T(1,128)S(1)}, u32[]{:S(2)}, u32[]{:S(2)}) collective-permute-start(s32[1,8]{1,0:T(1,128)S(1)} %get-tuple-element.65), channel_id=1, source_target_pairs={{0,96},{16,112},{32,64},{48,80},{64,32},{80,48},{96,0},{112,16},{1... | collective-permute-start | bytes 104 | tf_op jit(solution)/shard_map/ppermute | solution.py:18
  26.1 5.8 %collective-permute-done.1 = s32[1,8]{1,0:T(1,128)S(1)} collective-permute-done((s32[1,8]{1,0:T(1,128)S(1)}, s32[1,8]{1,0:T(1,128)S(1)}, u32[]{:S(2)}, u32[]{:S(2)}) %collective-permute-start.1) | collective-permute-done | bytes 64 | tf_op jit(solution)/shard_map/ppermute | solution.py:18
  31.9 1.3 collective-permute-start.6
  33.6 2.5 %collective-permute-done.6 = s32[1,8]{1,0:T(1,128)S(1)} collective-permute-done((s32[1,8]{1,0:T(1,128)S(1)}, s32[1,8]{1,0:T(1,128)S(1)}, u32[]{:S(2)}, u32[]{:S(2)}) %collective-permute-start.6) | collective-permute-done | bytes 64 | tf_op jit(solution)/shard_map/ppermute | solution.py:18
  36.2 2.6 %fusion.10 = f32[96,4096]{1,0:T(8,128)} fusion(f32[8,8,32,128]{3,2,1,0:T(8,128)S(1)} %all-to-all-done, s32[64]{0:T(128)S(1)} %eq.15), kind=kOutput, calls=%fused_computation.10 | convolution fusion | flops 301996032 | bytes 2621696 | tf_op jit(solution)/shard_map/dot_general | solution.py:67
  40.2 27.4 %all_gather.3 = bf16[32,12288]{1,0:T(8,128)(2,1)S(1)} all-gather(bf16[32,768]{1,0:T(8,128)(2,1)S(1)} %bitcast_multiply_fusion), channel_id=1, replica_groups=mesh['region'=8,'local'=16] {'local'}, dimensions={1}, use_global_device_ids=true | all-gather | bytes 835584 | tf_op jit(solution)/shard_map/all_gather | solution.py:45
  67.6 63.2 %all-reduce.3.cloned.1.call-done = f32[96,4096]{1,0:T(8,128)} async-done(((f32[96,4096]{1,0:T(8,128)}), f32[96,4096]{1,0:T(8,128)}) %all-reduce.3.cloned.1.call-update) | async-done | bytes 1572880
  130.8 1.0 constant_dynamic-slice_fusion.8
  131.8 9.6 %fusion.7 = f32[32,768]{1,0:T(8,128)S(1)} fusion(bf16[32,12288]{1,0:T(8,128)(2,1)S(1)} %all_gather.3, bf16[1,12288,768]{2,1,0:T(8,128)(2,1)} %param.15, f32[4,8,6,128]{3,2,1,0:T(8,128)S(1)} %bitcast.61), kind=kOutput, calls=%fused_computation.9 | convolution fusion | flops 604004352 | bytes 19857408 | tf_op jit(solution)/shard_map/dot_general | solution.py:44
  141.5 45.5 %while.14 = (s32[]{:T(128)}, f32[768]{0:T(1024)S(1)}, f32[768]{0:T(1024)S(1)}, f32[32,768]{1,0:T(8,128)}, f32[768]{0:T(1024)S(1)}, /*index=5*/f32[32,768]{1,0:T(8,128)S(1)}, f32[768]{0:T(1024)S(1)}, s32[]{:T(128)}, s32[]{:T(128)}) while((s32[]{:T(128)}, f32[768]{0:T(1024)S(1)}, f32[768]{0:T(1024)S(1)}, f32[32,768]{1,0:T(8,128)}, ...), condition=%wide.region_2.3_spmd, body=%wide.region_1.2_spmd.sunk | while | flops 6146 | bytes 40037 | solution.py:85
  141.6 1.4 dynamic_update_slice.37
  143.0 1.4 dynamic_update_slice.37
  144.4 1.4 dynamic_update_slice.37
  145.8 1.4 dynamic_update_slice.37
  147.2 1.4 dynamic_update_slice.37
  148.7 1.4 dynamic_update_slice.37
  150.1 1.4 dynamic_update_slice.37
  151.5 1.4 dynamic_update_slice.37
  152.9 1.4 dynamic_update_slice.37
  154.4 1.4 dynamic_update_slice.37
  155.8 1.4 dynamic_update_slice.37
  157.2 1.4 dynamic_update_slice.37
  158.6 1.4 dynamic_update_slice.37
  160.0 1.4 dynamic_update_slice.37
  161.5 1.4 dynamic_update_slice.37
  162.9 1.4 dynamic_update_slice.37
  164.3 1.4 dynamic_update_slice.37
  165.7 1.4 dynamic_update_slice.37
  167.2 1.4 dynamic_update_slice.37
  168.6 1.4 dynamic_update_slice.37
  170.0 1.4 dynamic_update_slice.37
  171.4 1.4 dynamic_update_slice.37
  172.8 1.4 dynamic_update_slice.37
  174.3 1.4 dynamic_update_slice.37
  175.7 1.4 dynamic_update_slice.37
  177.1 1.4 dynamic_update_slice.37
  178.5 1.4 dynamic_update_slice.37
  180.0 1.4 dynamic_update_slice.37
  181.4 1.4 dynamic_update_slice.37
  182.8 1.4 dynamic_update_slice.37
  184.2 1.4 dynamic_update_slice.37
  185.6 1.4 dynamic_update_slice.37
  (146 shorter events, 6.0 us)
Async XLA Ops:
  7.2 4.0 %copy-start = (bf16[1,1,8,8,128,128]{5,4,3,2,1,0:T(8,128)(2,1)S(1)}, bf16[1,1,8,8,128,128]{5,4,3,2,1,0:T(8,128)(2,1)}, u32[]{:S(2)}) copy-start(bf16[1,1,8,8,128,128]{5,4,3,2,1,0:T(8,128)(2,1)} %param.16) | copy-start | bytes 6291460
  11.1 6.4 %copy-start.7 = (s32[1,1,8,8]{3,2,1,0:T(8,128)S(1)}, s32[1,1,8,8]{3,2,1,0:T(8,128)}, u32[]{:S(2)}) copy-start(s32[1,1,8,8]{3,2,1,0:T(8,128)} %param.18) | copy-start | bytes 772
  12.8 23.3 %all-to-all-start = ((f32[8,8,32,128]{3,2,1,0:T(8,128)}), f32[8,8,32,128]{3,2,1,0:T(8,128)S(1)}, u32[]{:S(2)}, u32[]{:S(2)}) async-start(f32[8,8,32,128]{3,2,1,0:T(8,128)} %fusion.4), calls=%async_computation | async-start | bytes 2097152 | tf_op jit(solution)/shard_map/all_to_all | solution.py:59
  17.4 113.4 %all-reduce.3.cloned.1.call-start = ((), (), s32[]{:S(2)}) async-start(), calls=%async_computation.1 | async-start | bytes 3145728
  17.5 5.5 %collective-permute-start = (s32[1,8]{1,0:T(1,128)S(1)}, s32[1,8]{1,0:T(1,128)S(1)}, u32[]{:S(2)}, u32[]{:S(2)}) collective-permute-start(s32[1,8]{1,0:T(1,128)S(1)} %get-tuple-element.63), channel_id=1, source_target_pairs={{0,16},{16,0},{32,48},{48,32},{64,80},{80,64},{96,112},{112,96},{1... | collective-permute-start | bytes 104 | tf_op jit(solution)/shard_map/ppermute | solution.py:18
  18.0 13.8 %collective-permute-start.1 = (s32[1,8]{1,0:T(1,128)S(1)}, s32[1,8]{1,0:T(1,128)S(1)}, u32[]{:S(2)}, u32[]{:S(2)}) collective-permute-start(s32[1,8]{1,0:T(1,128)S(1)} %get-tuple-element.62), channel_id=1, source_target_pairs={{0,32},{16,48},{32,0},{48,16},{64,96},{80,112},{96,64},{112,80},{1... | collective-permute-start | bytes 104 | tf_op jit(solution)/shard_map/ppermute | solution.py:18
  19.7 13.5 %collective-permute-start.2 = (s32[1,8]{1,0:T(1,128)S(1)}, s32[1,8]{1,0:T(1,128)S(1)}, u32[]{:S(2)}, u32[]{:S(2)}) collective-permute-start(s32[1,8]{1,0:T(1,128)S(1)} %get-tuple-element.61), channel_id=1, source_target_pairs={{0,48},{16,32},{32,16},{48,0},{64,112},{80,96},{96,80},{112,64},{1... | collective-permute-start | bytes 104 | tf_op jit(solution)/shard_map/ppermute | solution.py:18
  19.7 13.8 %collective-permute-start.3 = (s32[1,8]{1,0:T(1,128)S(1)}, s32[1,8]{1,0:T(1,128)S(1)}, u32[]{:S(2)}, u32[]{:S(2)}) collective-permute-start(s32[1,8]{1,0:T(1,128)S(1)} %get-tuple-element.60), channel_id=1, source_target_pairs={{0,64},{16,80},{32,96},{48,112},{64,0},{80,16},{96,32},{112,48},{1... | collective-permute-start | bytes 104 | tf_op jit(solution)/shard_map/ppermute | solution.py:18
  22.9 10.6 %collective-permute-start.4 = (s32[1,8]{1,0:T(1,128)S(1)}, s32[1,8]{1,0:T(1,128)S(1)}, u32[]{:S(2)}, u32[]{:S(2)}) collective-permute-start(s32[1,8]{1,0:T(1,128)S(1)} %get-tuple-element.59), channel_id=1, source_target_pairs={{0,80},{16,64},{32,112},{48,96},{64,16},{80,0},{96,48},{112,32},{1... | collective-permute-start | bytes 104 | tf_op jit(solution)/shard_map/ppermute | solution.py:18
  23.1 10.5 %collective-permute-start.5 = (s32[1,8]{1,0:T(1,128)S(1)}, s32[1,8]{1,0:T(1,128)S(1)}, u32[]{:S(2)}, u32[]{:S(2)}) collective-permute-start(s32[1,8]{1,0:T(1,128)S(1)} %get-tuple-element.65), channel_id=1, source_target_pairs={{0,96},{16,112},{32,64},{48,80},{64,32},{80,48},{96,0},{112,16},{1... | collective-permute-start | bytes 104 | tf_op jit(solution)/shard_map/ppermute | solution.py:18
  31.9 4.2 %collective-permute-start.6 = (s32[1,8]{1,0:T(1,128)S(1)}, s32[1,8]{1,0:T(1,128)S(1)}, u32[]{:S(2)}, u32[]{:S(2)}) collective-permute-start(s32[1,8]{1,0:T(1,128)S(1)} %get-tuple-element.58), channel_id=1, source_target_pairs={{0,112},{16,96},{32,80},{48,64},{64,48},{80,32},{96,16},{112,0},{1... | collective-permute-start | bytes 104 | tf_op jit(solution)/shard_map/ppermute | solution.py:18
  36.2 2.7 %copy-start.8 = (u32[128]{0:T(128)S(1)}, u32[128]{0:T(128)}, u32[]{:S(2)}) copy-start(u32[128]{0:T(128)} %constant.67) | copy-start | bytes 1540
  36.2 4.0 %copy-start.2 = (bf16[32,768]{1,0:T(8,128)(2,1)S(1)}, bf16[32,768]{1,0:T(8,128)(2,1)}, u32[]{:S(2)}) copy-start(bf16[32,768]{1,0:T(8,128)(2,1)} %param.14) | copy-start | bytes 147460
  131.8 9.7 %copy-start.1 = (f32[768]{0:T(1024)S(1)}, f32[768]{0:T(1024)}, u32[]{:S(2)}) copy-start(f32[768]{0:T(1024)} %param.23) | copy-start | bytes 9220
  131.8 9.7 %copy-start.4 = (f32[768]{0:T(1024)S(1)}, f32[768]{0:T(1024)}, u32[]{:S(2)}) copy-start(f32[768]{0:T(1024)} %param.22) | copy-start | bytes 9220
  131.8 9.7 %copy-start.5 = (f32[768]{0:T(1024)S(1)}, f32[768]{0:T(1024)}, u32[]{:S(2)}) copy-start(f32[768]{0:T(1024)} %param.20) | copy-start | bytes 9220
  131.8 9.7 %copy-start.6 = (f32[768]{0:T(1024)S(1)}, f32[768]{0:T(1024)}, u32[]{:S(2)}) copy-start(f32[768]{0:T(1024)} %param.21) | copy-start | bytes 9220
  187.0 0.6 copy-start.3
Sparse Core Ops, SparseCore 0:
  38.9 91.8 all-reduce.2
